TPU v7x, 32 devices: a whole 2x2x4 slice. The times are simulated.
32 devices in a mesh: dp: 4 (over x, core), tensor: 8 (over z, y).
Axes of the slice: x: 2, y: 2, z: 4, core: 2. Of those that a mesh axis runs over, the one named last changes fastest.
Arguments:
- tokens: bfloat16 [12288, 1024], P(('dp', 'tensor')), may hold values from -6 to 6
- seq_ids: int32 [12288], P('dp'), may hold values from 0 to 11, as said below
- blk_ids: int32 [12288], P('dp'), may hold values from 0 to 11, as said below
- norm1_gain: bfloat16 [1024], P('dp'), may hold values from 0.099609375 to 1.8984375
- w_query: bfloat16 [1024, 1024], P('dp', 'tensor'), may hold values from -0.375 to 0.375
- w_key: bfloat16 [1024, 1024], P('dp', 'tensor'), may hold values from -0.1875 to 0.1875
- w_value: bfloat16 [1024, 1024], P('dp', 'tensor'), may hold values from -0.1875 to 0.1875
- w_out: bfloat16 [1024, 1024], P('tensor', 'dp'), may hold values from -0.75 to 0.75
- norm2_gain: bfloat16 [1024], P('dp'), may hold values from 0.099609375 to 1.8984375
- w_gate: bfloat16 [1024, 4096], P('dp', 'tensor'), may hold values from -0.1875 to 0.1875
- w_up: bfloat16 [1024, 4096], P('dp', 'tensor'), may hold values from -0.1875 to 0.1875
- w_down: bfloat16 [4096, 1024], P('tensor', 'dp'), may hold values from -0.09375 to 0.09375
- cotangent: bfloat16 [12288, 1024], P(('dp', 'tensor')), may hold values from -6 to 6
Outputs:
- output: bfloat16 [12288, 1024], P(('dp', 'tensor'))
- input_grad: bfloat16 [12288, 1024], P(('dp', 'tensor'))
- grad_query: float32 [1024, 1024], P('dp', 'tensor')
- grad_key: float32 [1024, 1024], P('dp', 'tensor')
- grad_value: float32 [1024, 1024], P('dp', 'tensor')
- grad_out: float32 [1024, 1024], P('tensor', 'dp')
- grad_gate: float32 [1024, 4096], P('dp', 'tensor')
- grad_up: float32 [1024, 4096], P('dp', 'tensor')
- grad_down: float32 [4096, 1024], P('tensor', 'dp')
- grad_norm1: float32 [1024], P(('dp', 'tensor'))
- grad_norm2: float32 [1024], P(('dp', 'tensor'))
Inputs may be any that keep to these rules, and one draw needn't show every extreme that they name: `seq_ids`: sequence ids never fall along the tokens; each sequence is a whole number of aligned runs of 1024 tokens and lies within one aligned run of 3072 tokens. `blk_ids`: the block index of a token is its position within its sequence divided by 256, rounded down.
All inputs are finite; a program needn't handle non-finite values.
Results may differ from a plain program's by a relative error of at most 0.02.
Values may be sent and summed in bfloat16 or wider, within the bound.
No kernel may reach another device: no remote copies, remote signals or barrier semaphores. Data moves between devices by JAX's collectives and lax.ppermute only.
A program may use at most 128 MiB of HBM per device.

v0:
```python
import jax
import jax.numpy as jnp
from jax import lax
from jax.sharding import PartitionSpec as P

DH = 64
EPS = 1e-06
NEG = -1e30


def row_scale(values):
    return lax.rsqrt(jnp.mean(values * values, axis=-1, keepdims=True) + EPS)


def norm_back(grad_normed, values, scale, gain):
    weighted = grad_normed * gain
    inner = jnp.mean(weighted * values, axis=-1, keepdims=True)
    grad_values = scale * weighted - values * (scale * scale * scale) * inner
    grad_gain = jnp.sum(grad_normed * values * scale, axis=0)
    return (grad_values, grad_gain)


def allowed_mask(seq_ids, blk_ids, start, count):
    query_seq = lax.dynamic_slice_in_dim(seq_ids, start, count, 0)
    query_blk = lax.dynamic_slice_in_dim(blk_ids, start, count, 0)
    return (query_seq[:, None] == seq_ids[None, :]) & (blk_ids[None, :] <= query_blk[:, None])


def attention_forward(queries, keys, values, seq_ids, blk_ids, factor):
    rows, heads, width = queries.shape
    block = min(512, rows)

    def one_block(start):
        query_block = lax.dynamic_slice_in_dim(queries, start, block, 0)
        allowed = allowed_mask(seq_ids, blk_ids, start, block)
        scores = (
            jnp.einsum("qhd,khd->hqk", query_block, keys, preferred_element_type=jnp.float32)
            * factor
        )
        scores = jnp.where(allowed[None], scores, NEG)
        highest = jnp.max(scores, axis=-1, keepdims=True)
        weights = jnp.exp(scores - highest)
        totals = jnp.sum(weights, axis=-1, keepdims=True)
        probs = (weights / totals).astype(jnp.bfloat16)
        mixed = jnp.einsum("hqk,khd->qhd", probs, values, preferred_element_type=jnp.float32)
        return (mixed.astype(jnp.bfloat16), (highest + jnp.log(totals))[..., 0])

    starts = jnp.arange(rows // block, dtype=jnp.int32) * block
    mixed, logsum = lax.map(one_block, starts)
    return (mixed.reshape(rows, heads * width), logsum)


def attention_backward(queries, keys, values, grad_mixed, logsum, seq_ids, blk_ids, factor):
    rows, heads, width = queries.shape
    block = min(512, rows)
    grad_heads = grad_mixed.reshape(rows, heads, width)

    def one_block(carry, inputs):
        start, block_logsum = inputs
        grad_keys, grad_values = carry
        query_block = lax.dynamic_slice_in_dim(queries, start, block, 0)
        grad_block = lax.dynamic_slice_in_dim(grad_heads, start, block, 0)
        allowed = allowed_mask(seq_ids, blk_ids, start, block)
        scores = (
            jnp.einsum("qhd,khd->hqk", query_block, keys, preferred_element_type=jnp.float32)
            * factor
        )
        scores = jnp.where(allowed[None], scores, NEG)
        probs = jnp.exp(scores - block_logsum[..., None])
        grad_probs = jnp.einsum(
            "qhd,khd->hqk", grad_block, values, preferred_element_type=jnp.float32
        )
        inner = jnp.sum(probs * grad_probs, axis=-1, keepdims=True)
        grad_scores = (probs * (grad_probs - inner)).astype(jnp.bfloat16)
        grad_query = (
            jnp.einsum("hqk,khd->qhd", grad_scores, keys, preferred_element_type=jnp.float32)
            * factor
        )
        grad_keys = (
            grad_keys
            + jnp.einsum(
                "hqk,qhd->khd", grad_scores, query_block, preferred_element_type=jnp.float32
            )
            * factor
        )
        grad_values = grad_values + jnp.einsum(
            "hqk,qhd->khd",
            probs.astype(jnp.bfloat16),
            grad_block,
            preferred_element_type=jnp.float32,
        )
        return ((grad_keys, grad_values), grad_query.astype(jnp.bfloat16))

    starts = jnp.arange(rows // block, dtype=jnp.int32) * block
    zeros = jnp.zeros((rows, heads, width), jnp.float32)
    (grad_keys, grad_values), grad_queries = lax.scan(one_block, (zeros, zeros), (starts, logsum))
    return (
        grad_queries.reshape(rows, heads * width),
        grad_keys.astype(jnp.bfloat16).reshape(rows, heads * width),
        grad_values.astype(jnp.bfloat16).reshape(rows, heads * width),
    )


def on_device(
    tokens,
    seq_ids,
    blk_ids,
    norm1_gain,
    w_query,
    w_key,
    w_value,
    w_out,
    norm2_gain,
    w_gate,
    w_up,
    w_down,
    cotangent,
):
    factor = DH ** (-0.5)
    gathered = (
        lax.all_gather(norm1_gain, "dp", axis=0, tiled=True),
        lax.all_gather(norm2_gain, "dp", axis=0, tiled=True),
        lax.all_gather(w_query, "dp", axis=0, tiled=True),
        lax.all_gather(w_key, "dp", axis=0, tiled=True),
        lax.all_gather(w_value, "dp", axis=0, tiled=True),
        lax.all_gather(w_out, "dp", axis=1, tiled=True),
        lax.all_gather(w_gate, "dp", axis=0, tiled=True),
        lax.all_gather(w_up, "dp", axis=0, tiled=True),
        lax.all_gather(w_down, "dp", axis=1, tiled=True),
    )
    (
        gain_first,
        gain_second,
        query_full,
        key_full,
        value_full,
        out_full,
        gate_full,
        up_full,
        down_full,
    ) = gathered
    resid = tokens.astype(jnp.float32)
    first_gain = gain_first.astype(jnp.float32)
    first_scale = row_scale(resid)
    normed_first = (resid * first_scale * first_gain).astype(jnp.bfloat16)
    group_first = lax.all_gather(normed_first, "tensor", axis=0, tiled=True)
    rows = group_first.shape[0]
    heads = query_full.shape[1] // DH
    queries = (
        jnp.dot(group_first, query_full, preferred_element_type=jnp.float32)
        .astype(jnp.bfloat16)
        .reshape(rows, heads, DH)
    )
    keys = (
        jnp.dot(group_first, key_full, preferred_element_type=jnp.float32)
        .astype(jnp.bfloat16)
        .reshape(rows, heads, DH)
    )
    values = (
        jnp.dot(group_first, value_full, preferred_element_type=jnp.float32)
        .astype(jnp.bfloat16)
        .reshape(rows, heads, DH)
    )
    attended, logsum = attention_forward(queries, keys, values, seq_ids, blk_ids, factor)
    piece = attended
    attn_total = lax.psum_scatter(
        jnp.dot(piece, out_full, preferred_element_type=jnp.float32),
        "tensor",
        scatter_dimension=0,
        tiled=True,
    )
    mixed = resid + attn_total
    second_gain = gain_second.astype(jnp.float32)
    second_scale = row_scale(mixed)
    normed_second = (mixed * second_scale * second_gain).astype(jnp.bfloat16)
    group_second = lax.all_gather(normed_second, "tensor", axis=0, tiled=True)
    gate = jnp.dot(group_second, gate_full, preferred_element_type=jnp.float32)
    upward = jnp.dot(group_second, up_full, preferred_element_type=jnp.float32)
    sigmoid_gate = jax.nn.sigmoid(gate)
    silu_gate = gate * sigmoid_gate
    hidden = (silu_gate * upward).astype(jnp.bfloat16)
    piece = hidden
    ffn_total = lax.psum_scatter(
        jnp.dot(piece, down_full, preferred_element_type=jnp.float32).astype(jnp.bfloat16),
        "tensor",
        scatter_dimension=0,
        tiled=True,
    ).astype(jnp.float32)
    output = (mixed + ffn_total).astype(jnp.bfloat16)
    back_params = (
        lax.all_gather(norm1_gain, "dp", axis=0, tiled=True),
        lax.all_gather(norm2_gain, "dp", axis=0, tiled=True),
        lax.all_gather(w_query, "dp", axis=0, tiled=True),
        lax.all_gather(w_key, "dp", axis=0, tiled=True),
        lax.all_gather(w_value, "dp", axis=0, tiled=True),
        lax.all_gather(w_out, "dp", axis=1, tiled=True),
        lax.all_gather(w_gate, "dp", axis=0, tiled=True),
        lax.all_gather(w_up, "dp", axis=0, tiled=True),
        lax.all_gather(w_down, "dp", axis=1, tiled=True),
    )
    (
        back_gain_first,
        back_gain_second,
        back_query,
        back_key,
        back_value,
        back_out,
        back_gate,
        back_up,
        back_down,
    ) = back_params
    first_gain_back = back_gain_first.astype(jnp.float32)
    second_gain_back = back_gain_second.astype(jnp.float32)
    grad_rows = lax.all_gather(cotangent, "tensor", axis=0, tiled=True)
    grad_hidden = jnp.einsum("tm,fm->tf", grad_rows, back_down, preferred_element_type=jnp.float32)
    grad_down_w = jnp.einsum("tf,tm->fm", hidden, grad_rows, preferred_element_type=jnp.float32)
    slope = sigmoid_gate * (1.0 + gate * (1.0 - sigmoid_gate))
    grad_gate = (grad_hidden * upward * slope).astype(jnp.bfloat16)
    grad_upward = (grad_hidden * silu_gate).astype(jnp.bfloat16)
    grad_gate_w = jnp.einsum(
        "tm,tf->mf", group_second, grad_gate, preferred_element_type=jnp.float32
    )
    grad_up_w = jnp.einsum(
        "tm,tf->mf", group_second, grad_upward, preferred_element_type=jnp.float32
    )
    first_part = jnp.einsum("tf,mf->tm", grad_gate, back_gate, preferred_element_type=jnp.float32)
    grad_normed_second = lax.psum_scatter(
        (
            first_part
            + jnp.einsum("tf,mf->tm", grad_upward, back_up, preferred_element_type=jnp.float32)
        ).astype(jnp.bfloat16),
        "tensor",
        scatter_dimension=0,
        tiled=True,
    ).astype(jnp.float32)
    grad_mixed_norm, grad_gain_second = norm_back(
        grad_normed_second, mixed, second_scale, second_gain_back
    )
    grad_mixed = cotangent.astype(jnp.float32) + grad_mixed_norm
    attn_grad_group = lax.all_gather(grad_mixed.astype(jnp.bfloat16), "tensor", axis=0, tiled=True)
    grad_attended = jnp.einsum(
        "tm,hm->th", attn_grad_group, back_out, preferred_element_type=jnp.float32
    ).astype(jnp.bfloat16)
    grad_out_w = jnp.einsum(
        "th,tm->hm", attended, attn_grad_group, preferred_element_type=jnp.float32
    )
    grad_queries, grad_keys, grad_values = attention_backward(
        queries, keys, values, grad_attended, logsum, seq_ids, blk_ids, factor
    )
    grad_query_w = jnp.einsum(
        "tm,th->mh", group_first, grad_queries, preferred_element_type=jnp.float32
    )
    grad_key_w = jnp.einsum("tm,th->mh", group_first, grad_keys, preferred_element_type=jnp.float32)
    grad_value_w = jnp.einsum(
        "tm,th->mh", group_first, grad_values, preferred_element_type=jnp.float32
    )
    summed = (
        lax.psum_scatter(
            grad_query_w.astype(jnp.bfloat16), "dp", scatter_dimension=0, tiled=True
        ).astype(jnp.float32),
        lax.psum_scatter(
            grad_key_w.astype(jnp.bfloat16), "dp", scatter_dimension=0, tiled=True
        ).astype(jnp.float32),
        lax.psum_scatter(
            grad_value_w.astype(jnp.bfloat16), "dp", scatter_dimension=0, tiled=True
        ).astype(jnp.float32),
        lax.psum_scatter(
            grad_out_w.astype(jnp.bfloat16), "dp", scatter_dimension=1, tiled=True
        ).astype(jnp.float32),
        lax.psum_scatter(
            grad_gate_w.astype(jnp.bfloat16), "dp", scatter_dimension=0, tiled=True
        ).astype(jnp.float32),
        lax.psum_scatter(
            grad_up_w.astype(jnp.bfloat16), "dp", scatter_dimension=0, tiled=True
        ).astype(jnp.float32),
        lax.psum_scatter(
            grad_down_w.astype(jnp.bfloat16), "dp", scatter_dimension=1, tiled=True
        ).astype(jnp.float32),
    )
    grad_query_w, grad_key_w, grad_value_w, grad_out_w, grad_gate_w, grad_up_w, grad_down_w = summed
    total = jnp.einsum("th,mh->tm", grad_queries, back_query, preferred_element_type=jnp.float32)
    total = total + jnp.einsum("th,mh->tm", grad_keys, back_key, preferred_element_type=jnp.float32)
    grad_normed_first = lax.psum_scatter(
        (
            total
            + jnp.einsum("th,mh->tm", grad_values, back_value, preferred_element_type=jnp.float32)
        ).astype(jnp.bfloat16),
        "tensor",
        scatter_dimension=0,
        tiled=True,
    ).astype(jnp.float32)
    grad_tokens_norm, grad_gain_first = norm_back(
        grad_normed_first, resid, first_scale, first_gain_back
    )
    input_grad = (grad_mixed + grad_tokens_norm).astype(jnp.bfloat16)
    grad_norm_first, grad_norm_second = (
        lax.psum_scatter(grad_gain_first, ("dp", "tensor"), scatter_dimension=0, tiled=True),
        lax.psum_scatter(grad_gain_second, ("dp", "tensor"), scatter_dimension=0, tiled=True),
    )
    return (
        output,
        input_grad,
        grad_query_w,
        grad_key_w,
        grad_value_w,
        grad_out_w,
        grad_gate_w,
        grad_up_w,
        grad_down_w,
        grad_norm_first,
        grad_norm_second,
    )


def solution(mesh):
    return jax.shard_map(
        on_device,
        mesh=mesh,
        in_specs=(
            P(("dp", "tensor"), None),
            P("dp"),
            P("dp"),
            P("dp"),
            P("dp", "tensor"),
            P("dp", "tensor"),
            P("dp", "tensor"),
            P("tensor", "dp"),
            P("dp"),
            P("dp", "tensor"),
            P("dp", "tensor"),
            P("tensor", "dp"),
            P(("dp", "tensor"), None),
        ),
        out_specs=(
            P(("dp", "tensor"), None),
            P(("dp", "tensor"), None),
            P("dp", "tensor"),
            P("dp", "tensor"),
            P("dp", "tensor"),
            P("tensor", "dp"),
            P("dp", "tensor"),
            P("dp", "tensor"),
            P("tensor", "dp"),
            P(("dp", "tensor")),
            P(("dp", "tensor")),
        ),
        check_vma=False,
    )
```

profile of v0, /device:TPU:0, one launch (start us, length us, event | category | flops | bytes accessed | tf_op | source)
XLA Modules:
  0.0 1455.7 jit_solution(128816638901233754)
XLA Ops:
  10.7 6.0 all-gather
  19.0 6.5 all_gather.50
  25.5 6.1 all_gather.51
  31.6 6.1 all_gather.52
  37.7 6.1 all_gather.53
  43.7 76.2 %all-gather.10.cloned.1.call-done = bf16[3072,1024]{1,0:T(8,128)(2,1)} async-done(((bf16[384,1024]{1,0:T(8,128)(2,1)}), bf16[3072,1024]{1,0:T(8,128)(2,1)}) %all-gather.10.cloned.1.call-update) | async-done | bytes 6291472 | tf_op jit(solution)/shard_map/all_gather | solution.py:146
  119.9 5.1 convolution_convert_fusion.2
  129.7 88.6 %while.27 = (s32[]{:T(128)}, bf16[6,512,2,64]{1,3,2,0:T(8,128)(2,1)S(1)}, f32[6,2,512]{2,1,0:T(2,128)S(1)}, s32[6]{0:T(128)S(1)}, s32[3072]{0:T(1024)S(1)}, /*in...) while((s32[]{:T(128)}, ...), condition=%wide.region_4.5_spmd, body=%wide.region_1.4_spmd.sunk | while | flops 847838208 | bytes 45945020 | solution.py:49
  219.1 6.4 fusion.58
  231.2 200.0 %reduce-scatter.12.cloned.1.call-done = f32[384,1024]{1,0:T(8,128)} async-done(((f32[3072,1024]{1,0:T(8,128)}), f32[384,1024]{1,0:T(8,128)}) %reduce-scatter.12.cloned.1.call-update) | async-done | bytes 1572880 | tf_op jit(solution)/shard_map/reduce_scatter | solution.py:166
  436.8 95.5 %all-gather.12.cloned.1.call-done = bf16[3072,1024]{1,0:T(8,128)(2,1)} async-done(((bf16[384,1024]{1,0:T(8,128)(2,1)}), bf16[3072,1024]{1,0:T(8,128)(2,1)}) %all-gather.12.cloned.1.call-update) | async-done | bytes 6291472 | tf_op jit(solution)/shard_map/all_gather | solution.py:176
  532.3 9.1 fusion.60
  541.5 7.1 all-gather.14.cloned.1.call-done
  548.5 9.1 fusion.59
  557.6 9.2 all-gather.18.cloned.1.call-done
  566.8 101.0 %all-gather.20.cloned.1.call-done = bf16[3072,1024]{1,0:T(8,128)(2,1)} async-done(((bf16[384,1024]{1,0:T(8,128)(2,1)}), bf16[3072,1024]{1,0:T(8,128)(2,1)}) %all-gather.20.cloned.1.call-update) | async-done | bytes 6291472 | tf_op jit(solution)/shard_map/all_gather | solution.py:214
  667.8 14.8 %multiply_convert_fusion.1 = (bf16[3072,512]{1,0:T(8,128)(2,1)}, bf16[3072,512]{1,0:T(8,128)(2,1)}, bf16[3072,512]{1,0:T(8,128)(2,1)}) fusion(f32[3072,512]{1,0:T(8,128)} %fusion.59, f32[3072,512]{1,0:T(8,128)} %fusion.60, bf16[3072,1024]{1,0:T(8,128)(2,1)} %all-gather.20.cloned.1.call-done, bf16[512,1024]{1,0:T(8,128)(2,1)} %all-gather.18.cloned.1.call-done), kind=kOutput, calls=%fused_computation.47 | convolution fusion | flops 3244818432 | bytes 29360128 | tf_op jit(solution)/shard_map/tm,fm->tf/dot_general | solution.py:215
  682.7 5.7 fusion.61
  688.4 7.7 add_convert_fusion.1
  696.1 115.9 %reduce-scatter.16.cloned.1.call-done = bf16[384,1024]{1,0:T(8,128)(2,1)} async-done(((bf16[3072,1024]{1,0:T(8,128)(2,1)}), bf16[384,1024]{1,0:T(8,128)(2,1)}) %reduce-scatter.16.cloned.1.call-update) | async-done | bytes 786448 | tf_op jit(solution)/shard_map/reduce_scatter | solution.py:227
  817.6 8.1 convolution_convert_fusion.5
  826.0 8.2 convolution_convert_fusion.6
  834.3 8.2 convolution_convert_fusion.7
  842.6 73.4 %all-gather.22.cloned.1.call-done = bf16[3072,1024]{1,0:T(8,128)(2,1)} async-done(((bf16[384,1024]{1,0:T(8,128)(2,1)}), bf16[3072,1024]{1,0:T(8,128)(2,1)}) %all-gather.22.cloned.1.call-update) | async-done | bytes 6291472 | tf_op jit(solution)/shard_map/all_gather | solution.py:240
  920.8 5.9 convolution_convert_fusion.1
  927.7 201.2 %while.28 = (s32[]{:T(128)}, f32[3072,2,64]{0,2,1:T(8,128)S(1)}, f32[3072,2,64]{0,2,1:T(8,128)}, bf16[6,512,2,64]{1,3,2,0:T(8,128)(2,1)}, s32[6]{0:T(128)S(1)}, ...) while((s32[]{:T(128)}, f32[3072,2,64]{0,2,1:T(8,128)S(1)}, ...), condition=%wide.region_12.13_spmd.clone, body=%wide.region_10.12_spmd.clone.sunk | while | flops 2067266560 | bytes 122618160 | solution.py:96
  939.9 8.9 multiply_reduce_fusion.3
  948.8 7.5 multiply_convert_fusion.6
  973.3 8.9 multiply_reduce_fusion.3
  982.3 7.5 multiply_convert_fusion.6
  1006.8 8.9 multiply_reduce_fusion.3
  1015.7 7.5 multiply_convert_fusion.6
  1040.3 8.9 multiply_reduce_fusion.3
  1049.2 7.5 multiply_convert_fusion.6
  1073.8 8.9 multiply_reduce_fusion.3
  1082.7 7.5 multiply_convert_fusion.6
  1107.2 8.9 multiply_reduce_fusion.3
  1116.1 7.5 multiply_convert_fusion.6
  1131.8 5.5 convolution_convert_fusion.11
  1137.3 7.6 fusion.63
  1147.7 6.4 fusion.62
  1154.2 5.3 convolution_convert_fusion.9
  1159.6 12.2 add_convert_fusion
  1173.0 7.6 convolution_convert_fusion
  1190.8 10.3 reduce-scatter.24.cloned.1.call-done
  1202.6 120.1 %reduce-scatter.18.cloned.1.call-done = bf16[384,1024]{1,0:T(8,128)(2,1)} async-done(((bf16[3072,1024]{1,0:T(8,128)(2,1)}), bf16[384,1024]{1,0:T(8,128)(2,1)}) %reduce-scatter.18.cloned.1.call-update) | async-done | bytes 786448 | tf_op jit(solution)/shard_map/reduce_scatter | solution.py:283
  1324.4 42.2 %all-reduce.2 = (f32[1024]{0:T(1024)S(1)}, f32[1024]{0:T(1024)S(1)}) all-reduce(f32[1024]{0:T(1024)S(1)} %get-tuple-element.169, f32[1024]{0:T(1024)S(1)} %copy-done.31), channel_id=13, replica_groups=mesh['dp'=4,'tensor'=8] {'dp','tensor'}, use_global_device_ids=true, to_apply=%region_23.24.clone | all-reduce | flops 2048 | bytes 16384
  1367.8 76.8 %reduce-scatter.14.cloned.1.call-done = bf16[384,1024]{1,0:T(8,128)(2,1)} async-done(((bf16[3072,1024]{1,0:T(8,128)(2,1)}), bf16[384,1024]{1,0:T(8,128)(2,1)}) %reduce-scatter.14.cloned.1.call-update) | async-done | bytes 786448 | tf_op jit(solution)/shard_map/reduce_scatter | solution.py:183
  (286 shorter events, 224.7 us)
Async XLA Ops:
  8.0 111.9 %all-gather.10.cloned.1.call-start = ((), (), s32[]{:S(2)}) async-start(), calls=%async_computation.11 | async-start | bytes 7077888 | tf_op jit(solution)/shard_map/all_gather | solution.py:146
  10.7 14.8 %copy-start.25 = (f32[384]{0:T(512)}, f32[384]{0:T(512)S(1)}, u32[]{:S(2)}) copy-start(f32[384]{0:T(512)S(1)} %get-tuple-element.227) | copy-start | bytes 4612
  16.7 8.8 copy-start.21
  19.0 412.2 %reduce-scatter.12.cloned.1.call-start = ((), (), s32[]{:S(2)}) async-start(), calls=%async_computation.12 | async-start | bytes 14155776 | tf_op jit(solution)/shard_map/reduce_scatter | solution.py:166
  25.5 101.8 %copy-start.10 = (bf16[1024,128]{1,0:T(8,128)(2,1)}, bf16[1024,128]{1,0:T(8,128)(2,1)S(1)}, u32[]{:S(2)}) copy-start(bf16[1024,128]{1,0:T(8,128)(2,1)S(1)} %all_gather.50) | copy-start | bytes 786436
  31.6 93.5 %copy-start.12 = (bf16[1024,128]{1,0:T(8,128)(2,1)}, bf16[1024,128]{1,0:T(8,128)(2,1)S(1)}, u32[]{:S(2)}) copy-start(bf16[1024,128]{1,0:T(8,128)(2,1)S(1)} %all_gather.51) | copy-start | bytes 786436
  37.7 82.3 %copy-start.8 = (bf16[1024,128]{1,0:T(8,128)(2,1)}, bf16[1024,128]{1,0:T(8,128)(2,1)S(1)}, u32[]{:S(2)}) copy-start(bf16[1024,128]{1,0:T(8,128)(2,1)S(1)} %all_gather.52) | copy-start | bytes 786436
  225.4 211.4 %all-gather.16.cloned.1.call-start = ((), (), s32[]{:S(2)}) async-start(), calls=%async_computation.15 | async-start | bytes 1310720 | tf_op jit(solution)/shard_map/all_gather | solution.py:128
  226.0 306.3 %all-gather.12.cloned.1.call-start = ((), (), s32[]{:S(2)}) async-start(), calls=%async_computation.13 | async-start | bytes 7077888 | tf_op jit(solution)/shard_map/all_gather | solution.py:176
  231.2 583.1 %copy-start.19 = (f32[4,1,256]{2,1,0:T(1,128)}, f32[4,1,256]{2,1,0:T(1,128)S(1)}, u32[]{:S(2)}) copy-start(f32[4,1,256]{2,1,0:T(1,128)S(1)} %convert_element_type.176) | copy-start | bytes 12292
  433.1 381.2 %copy-start.1 = (f32[384,1024]{1,0:T(8,128)}, f32[384,1024]{1,0:T(8,128)S(1)}, u32[]{:S(2)}) copy-start(f32[384,1024]{1,0:T(8,128)S(1)} %get-tuple-element.216) | copy-start | bytes 4718596
  433.1 381.2 %copy-start.23 = (f32[384]{0:T(512)}, f32[384]{0:T(512)S(1)}, u32[]{:S(2)}) copy-start(f32[384]{0:T(512)S(1)} %get-tuple-element.229) | copy-start | bytes 4612
  433.1 381.2 %copy-start.27 = (f32[384]{0:T(512)}, f32[384]{0:T(512)S(1)}, u32[]{:S(2)}) copy-start(f32[384]{0:T(512)S(1)} %get-tuple-element.228) | copy-start | bytes 4612
  434.4 114.1 %all-gather.14.cloned.1.call-start = ((), (), s32[]{:S(2)}) async-start(), calls=%async_computation.14 | async-start | bytes 1310720 | tf_op jit(solution)/shard_map/all_gather | solution.py:127
  435.0 131.9 %all-gather.18.cloned.1.call-start = ((), (), s32[]{:S(2)}) async-start(), calls=%async_computation.16 | async-start | bytes 1310720 | tf_op jit(solution)/shard_map/all_gather | solution.py:129
  435.7 232.1 %all-gather.20.cloned.1.call-start = ((), (), s32[]{:S(2)}) async-start(), calls=%async_computation.18 | async-start | bytes 7077888 | tf_op jit(solution)/shard_map/all_gather | solution.py:214
  436.5 375.5 %reduce-scatter.16.cloned.1.call-start = ((), (), s32[]{:S(2)}) async-start(), calls=%async_computation.19 | async-start | bytes 7077888 | tf_op jit(solution)/shard_map/reduce_scatter | solution.py:227
  667.8 14.8 %copy-start.35 = (bf16[1024,512]{1,0:T(8,128)(2,1)S(1)}, bf16[1024,512]{1,0:T(8,128)(2,1)}, u32[]{:S(2)}) copy-start(bf16[1024,512]{1,0:T(8,128)(2,1)} %all-gather.14.cloned.1.call-done) | copy-start | bytes 3145732
  696.1 219.9 %all-gather.22.cloned.1.call-start = ((), (), s32[]{:S(2)}) async-start(), calls=%async_computation.20 | async-start | bytes 7077888 | tf_op jit(solution)/shard_map/all_gather | solution.py:240
  817.6 363.2 %reduce-scatter.32.cloned.1.call-start = ((), (), s32[]{:S(2)}) async-start(), calls=%async_computation.28 | async-start | bytes 1310720 | tf_op jit(solution)/shard_map/reduce_scatter | solution.py:276
  825.8 356.9 %reduce-scatter.30.cloned.1.call-start = ((), (), s32[]{:S(2)}) async-start(), calls=%async_computation.27 | async-start | bytes 1310720 | tf_op jit(solution)/shard_map/reduce_scatter | solution.py:273
  834.3 350.2 %reduce-scatter.28.cloned.1.call-start = ((), (), s32[]{:S(2)}) async-start(), calls=%async_computation.26 | async-start | bytes 1310720 | tf_op jit(solution)/shard_map/reduce_scatter | solution.py:270
  842.5 343.8 %reduce-scatter.26.cloned.1.call-start = ((), (), s32[]{:S(2)}) async-start(), calls=%async_computation.25 | async-start | bytes 327680 | tf_op jit(solution)/shard_map/reduce_scatter | solution.py:267
  920.8 267.1 %reduce-scatter.20.cloned.1.call-start = ((), (), s32[]{:S(2)}) async-start(), calls=%async_computation.22 | async-start | bytes 327680 | tf_op jit(solution)/shard_map/reduce_scatter | solution.py:258
  939.8 8.9 copy-start.17
  973.3 8.9 copy-start.17
  1006.8 8.9 copy-start.17
  1040.3 8.9 copy-start.17
  1073.8 8.9 copy-start.17
  1107.2 8.9 copy-start.17
  1131.8 13.2 slice-start
  1137.3 52.0 %reduce-scatter.22.cloned.1.call-start = ((), (), s32[]{:S(2)}) async-start(), calls=%async_computation.23 | async-start | bytes 327680 | tf_op jit(solution)/shard_map/reduce_scatter | solution.py:261
  1137.3 7.7 slice-start.1
  1137.3 7.7 copy-start.7
  1147.6 53.5 %reduce-scatter.24.cloned.1.call-start = ((), (), s32[]{:S(2)}) async-start(), calls=%async_computation.24 | async-start | bytes 327680 | tf_op jit(solution)/shard_map/reduce_scatter | solution.py:264
  1159.5 163.2 %reduce-scatter.18.cloned.1.call-start = ((), (), s32[]{:S(2)}) async-start(), calls=%async_computation.21 | async-start | bytes 7077888 | tf_op jit(solution)/shard_map/reduce_scatter | solution.py:283
  1171.8 272.8 %reduce-scatter.14.cloned.1.call-start = ((), (), s32[]{:S(2)}) async-start(), calls=%async_computation.17 | async-start | bytes 7077888 | tf_op jit(solution)/shard_map/reduce_scatter | solution.py:183
  1180.6 142.1 %copy-start.3 = (bf16[384,1024]{1,0:T(8,128)(2,1)S(1)}, bf16[384,1024]{1,0:T(8,128)(2,1)}, u32[]{:S(2)}) copy-start(bf16[384,1024]{1,0:T(8,128)(2,1)} %param.17) | copy-start | bytes 2359300
  1180.6 142.1 %copy-start.22 = (f32[4,1,256]{2,1,0:T(1,128)S(1)}, f32[4,1,256]{2,1,0:T(1,128)}, u32[]{:S(2)}) copy-start(f32[4,1,256]{2,1,0:T(1,128)} %copy-done.21) | copy-start | bytes 12292
  1180.6 142.1 %copy-start.26 = (f32[384]{0:T(512)S(1)}, f32[384]{0:T(512)}, u32[]{:S(2)}) copy-start(f32[384]{0:T(512)} %copy-done.25) | copy-start | bytes 4612
  1180.6 143.8 %copy-start.31 = (f32[1024]{0:T(1024)S(1)}, f32[1024]{0:T(1024)}, u32[]{:S(2)}) copy-start(f32[1024]{0:T(1024)} %get-tuple-element.167) | copy-start | bytes 12292
  1180.6 264.0 %copy-start.2 = (f32[384,1024]{1,0:T(8,128)S(1)}, f32[384,1024]{1,0:T(8,128)}, u32[]{:S(2)}) copy-start(f32[384,1024]{1,0:T(8,128)} %copy-done.1) | copy-start | bytes 4718596
  1180.6 264.0 %copy-start.6 = (bf16[384,1024]{1,0:T(8,128)(2,1)S(1)}, bf16[384,1024]{1,0:T(8,128)(2,1)}, u32[]{:S(2)}) copy-start(bf16[384,1024]{1,0:T(8,128)(2,1)} %param.29) | copy-start | bytes 2359300
  1180.6 264.0 %copy-start.20 = (f32[4,1,256]{2,1,0:T(1,128)S(1)}, f32[4,1,256]{2,1,0:T(1,128)}, u32[]{:S(2)}) copy-start(f32[4,1,256]{2,1,0:T(1,128)} %copy-done.19) | copy-start | bytes 12292
  1180.7 264.0 %copy-start.24 = (f32[384]{0:T(512)S(1)}, f32[384]{0:T(512)}, u32[]{:S(2)}) copy-start(f32[384]{0:T(512)} %copy-done.23) | copy-start | bytes 4612
  1180.7 264.0 %copy-start.28 = (f32[384]{0:T(512)S(1)}, f32[384]{0:T(512)}, u32[]{:S(2)}) copy-start(f32[384]{0:T(512)} %copy-done.27) | copy-start | bytes 4612
  1180.7 264.0 %copy-start.30 = (f32[384]{0:T(512)S(1)}, f32[384]{0:T(512)}, u32[]{:S(2)}) copy-start(f32[384]{0:T(512)} %copy-done.29) | copy-start | bytes 4612
  1180.7 264.0 %copy-start.32 = (f32[384]{0:T(512)S(1)}, f32[384]{0:T(512)}, u32[]{:S(2)}) copy-start(f32[384]{0:T(512)} %get-tuple-element.226) | copy-start | bytes 4612
  (19 other events, 70.8 us)
Sparse Core Ops, SparseCore 0:
  19.1 100.8 all-gather.9
  225.6 205.5 reduce-scatter.11
  817.7 98.2 all-gather.21
Sparse Core Ops, SparseCore 1:
  227.5 14.8 all-gather.15
  434.5 97.8 all-gather.11
  533.8 14.7 all-gather.13
  550.1 16.7 all-gather.17
  569.1 98.7 all-gather.19
  696.2 115.8 reduce-scatter.15
  825.9 24.1 reduce-scatter.31
  852.5 24.8 reduce-scatter.29
  879.8 24.9 reduce-scatter.27
  920.8 18.2 reduce-scatter.25
  1137.3 18.1 reduce-scatter.19
  1158.7 20.0 reduce-scatter.21
  1181.1 20.0 reduce-scatter.23
  1205.1 117.5 reduce-scatter.17
  1326.7 117.8 reduce-scatter.13
where the time goes:
time: 1460 us
  waiting for transfers between devices  888 us (61%)
  matrix products  316 us (22%)
  other arithmetic  115 us (8%)
  blocking collectives  77.9 us (5%)
  loops' own time  24.7 us (2%)
  between operations  16.6 us (1%)
  local copies, waits for them, and re-layouts  16.3 us (1%)
    reduce_scatter x1, waiting for transfers between devices, on_device(): lax.psum_scatter(jnp.dot(piece, out_full, preferred_element_type=jnp.floa...  200 us
    reduce_scatter x1, waiting for transfers between devices, on_device(): lax.psum_scatter((total + jnp.einsum('th,mh->tm', grad_values, back_value...  120 us
    reduce_scatter x1, waiting for transfers between devices, on_device(): lax.psum_scatter((first_part + jnp.einsum('tf,mf->tm', grad_upward, back_...  116 us
    all_gather x1, waiting for transfers between devices, on_device(): grad_rows = lax.all_gather(cotangent, 'tensor', axis=0, tiled=True)  101 us
    all_gather x1, waiting for transfers between devices, on_device(): group_second = lax.all_gather(normed_second, 'tensor', axis=0, tiled=True)  95.5 us
    reduce_scatter x1, waiting for transfers between devices, on_device(): lax.psum_scatter(jnp.dot(piece, down_full, preferred_element_type=jnp.flo...  76.8 us
    all_gather x1, waiting for transfers between devices, on_device(): group_first = lax.all_gather(normed_first, 'tensor', axis=0, tiled=True)  76.2 us
    all_gather x1, waiting for transfers between devices, on_device(): lax.all_gather(grad_mixed.astype(jnp.bfloat16), 'tensor', axis=0, tiled=T...  73.4 us
  transfers between devices with their start and end apart: 18, of which 11 were waited for; matrix products, arithmetic and copies ran while one was open for 21% of the time, Pallas kernels for 0%

commit v1 on v0

--- a/solution.py
+++ b/solution.py
@@ -173,7 +173,31 @@
     second_gain = gain_second.astype(jnp.float32)
     second_scale = row_scale(mixed)
     normed_second = (mixed * second_scale * second_gain).astype(jnp.bfloat16)
-    group_second = lax.all_gather(normed_second, "tensor", axis=0, tiled=True)
+    size, index, rows_2 = (
+        lax.axis_size("tensor"),
+        lax.axis_index("tensor"),
+        normed_second.shape[0],
+    )
+    right = [(i, (i + 1) % size) for i in range(size)]
+    left = [(i, (i - 1) % size) for i in range(size)]
+    whole = jnp.zeros(
+        (*normed_second.shape[:0], size * rows_2, *normed_second.shape[0 + 1 :]),
+        normed_second.dtype,
+    )
+    whole = lax.dynamic_update_slice_in_dim(whole, normed_second, index * rows_2, axis=0)
+    from_left = from_right = normed_second
+    half = size // 2
+    for turn in range(1, half + 1):
+        from_left = lax.ppermute(from_left, "tensor", right)
+        whole = lax.dynamic_update_slice_in_dim(
+            whole, from_left, (index - turn) % size * rows_2, axis=0
+        )
+        if turn < size - half:
+            from_right = lax.ppermute(from_right, "tensor", left)
+            whole = lax.dynamic_update_slice_in_dim(
+                whole, from_right, (index + turn) % size * rows_2, axis=0
+            )
+    group_second = whole
     gate = jnp.dot(group_second, gate_full, preferred_element_type=jnp.float32)
     upward = jnp.dot(group_second, up_full, preferred_element_type=jnp.float32)
     sigmoid_gate = jax.nn.sigmoid(gate)

time: 1460 us -> 1410 us (0.966)
  waiting for transfers between devices: 888 us -> 807 us
  local copies, waits for them, and re-layouts: 16.3 us -> 33.3 us
  starting transfers between devices: 1.19 us -> 17.7 us
    all_gather x1, waiting for transfers between devices: 101 us -> 0.01 us  [on_device(): grad_rows = lax.all_gather(cotangent, 'tensor', axis=0, tiled=True)]
    all_gather x1 -> x0, waiting for transfers between devices: 95.5 us -> none  [on_device(): group_second = lax.all_gather(normed_second, 'tensor', axis=0, tiled=True)]
    ppermute x0 -> x7, waiting for transfers between devices: none -> 89.5 us  [the longest x4 89.5 us: on_device(): from_left = lax.ppermute(from_left, 'tensor', right)]
    reduce_scatter x1, waiting for transfers between devices: 200 us -> 244 us  [on_device(): lax.psum_scatter(jnp.dot(piece, out_full, preferred_element_type=jnp.floa...]
    ppermute x0 -> x7, starting transfers between devices: none -> 16.8 us  [the longest x4 9.24 us: on_device(): from_left = lax.ppermute(from_left, 'tensor', right)]
  transfers between devices with their start and end apart: 18 -> 24, of which waited for: 11 -> 11; matrix products, arithmetic and copies ran while one was open for 21% -> 23% of each run, Pallas kernels for 0% -> 0%
where the time goes in v1:
time: 1410 us; the launch traced here: 1400 us
  waiting for transfers between devices  807 us (57%)
  matrix products  313 us (22%)
  other arithmetic  115 us (8%)
  blocking collectives  77.8 us (6%)
  local copies, waits for them, and re-layouts  33.3 us (2%)
  loops' own time  25.1 us (2%)
  starting transfers between devices  17.7 us (1%)
  between operations  16.7 us (1%)
    reduce_scatter x1, waiting for transfers between devices, on_device(): lax.psum_scatter(jnp.dot(piece, out_full, preferred_element_type=jnp.floa...  244 us
    reduce_scatter x1, waiting for transfers between devices, on_device(): lax.psum_scatter((total + jnp.einsum('th,mh->tm', grad_values, back_value...  120 us
    reduce_scatter x1, waiting for transfers between devices, on_device(): lax.psum_scatter((first_part + jnp.einsum('tf,mf->tm', grad_upward, back_...  115 us
    ppermute x4, waiting for transfers between devices, on_device(): from_left = lax.ppermute(from_left, 'tensor', right)  89.5 us
    reduce_scatter x1, waiting for transfers between devices, on_device(): lax.psum_scatter(jnp.dot(piece, down_full, preferred_element_type=jnp.flo...  77 us
    all_gather x1, waiting for transfers between devices, on_device(): group_first = lax.all_gather(normed_first, 'tensor', axis=0, tiled=True)  76.2 us
    all_gather x1, waiting for transfers between devices, on_device(): lax.all_gather(grad_mixed.astype(jnp.bfloat16), 'tensor', axis=0, tiled=T...  73.2 us
    dot_general x6, matrix products, one_block(): jnp.einsum('qhd,khd->hqk', grad_block, values, preferred_element_type=jnp...  53.4 us
  transfers between devices with their start and end apart: 24, of which 11 were waited for; matrix products, arithmetic and copies ran while one was open for 23% of the time, Pallas kernels for 0%

profile of v1, /device:TPU:0, one launch (start us, length us, event | category | flops | bytes accessed | tf_op | source)
XLA Modules:
  0.0 1405.0 jit_solution(15061850655788084513)
XLA Ops:
  10.7 6.0 all-gather
  19.0 6.5 all_gather.47
  25.5 6.1 all_gather.48
  31.6 6.1 all_gather.49
  37.7 6.1 all_gather.50
  43.7 76.2 %all-gather.9.cloned.1.call-done = bf16[3072,1024]{1,0:T(8,128)(2,1)} async-done(((bf16[384,1024]{1,0:T(8,128)(2,1)}), bf16[3072,1024]{1,0:T(8,128)(2,1)}) %all-gather.9.cloned.1.call-update) | async-done | bytes 6291472 | tf_op jit(solution)/shard_map/all_gather | solution.py:146
  119.9 5.1 convolution_convert_fusion.2
  129.7 88.9 %while.27 = (s32[]{:T(128)}, bf16[6,512,2,64]{1,3,2,0:T(8,128)(2,1)S(1)}, f32[6,2,512]{2,1,0:T(2,128)S(1)}, s32[6]{0:T(128)S(1)}, s32[3072]{0:T(1024)S(1)}, /*in...) while((s32[]{:T(128)}, ...), condition=%wide.region_4.5_spmd, body=%wide.region_1.4_spmd.sunk | while | flops 847838208 | bytes 45945020 | solution.py:49
  219.3 6.4 fusion.58
  227.6 5.1 all-gather.1
  232.6 244.0 %reduce-scatter.12.cloned.1.call-done = f32[384,1024]{1,0:T(8,128)} async-done(((f32[3072,1024]{1,0:T(8,128)}), f32[384,1024]{1,0:T(8,128)}) %reduce-scatter.12.cloned.1.call-update) | async-done | bytes 1572880 | tf_op jit(solution)/shard_map/reduce_scatter | solution.py:166
  487.9 30.5 %collective-permute-done = bf16[384,1024]{1,0:T(8,128)(2,1)} collective-permute-done((bf16[384,1024]{1,0:T(8,128)(2,1)S(1)}, bf16[384,1024]{1,0:T(8,128)(2,1)}, u32[]{:S(2)}, u32[]{:S(2)}) %collective-permute-start) | collective-permute-done | bytes 786464 | tf_op jit(solution)/shard_map/ppermute | solution.py:191
  523.4 30.9 %collective-permute-done.2 = bf16[384,1024]{1,0:T(8,128)(2,1)} collective-permute-done((bf16[384,1024]{1,0:T(8,128)(2,1)}, bf16[384,1024]{1,0:T(8,128)(2,1)}, u32[]{:S(2)}, u32[]{:S(2)}) %collective-permute-start.2) | collective-permute-done | bytes 786464 | tf_op jit(solution)/shard_map/ppermute | solution.py:191
  559.0 9.2 fusion.60
  568.2 21.7 %collective-permute-done.4 = bf16[384,1024]{1,0:T(8,128)(2,1)} collective-permute-done((bf16[384,1024]{1,0:T(8,128)(2,1)}, bf16[384,1024]{1,0:T(8,128)(2,1)}, u32[]{:S(2)}, u32[]{:S(2)}) %collective-permute-start.4) | collective-permute-done | bytes 786464 | tf_op jit(solution)/shard_map/ppermute | solution.py:191
  605.2 6.3 collective-permute-done.6
  612.4 9.2 fusion.59
  621.6 13.5 multiply_convert_fusion.1
  638.5 7.7 add_convert_fusion.1
  646.5 114.7 %reduce-scatter.16.cloned.1.call-done = bf16[384,1024]{1,0:T(8,128)(2,1)} async-done(((bf16[3072,1024]{1,0:T(8,128)(2,1)}), bf16[384,1024]{1,0:T(8,128)(2,1)}) %reduce-scatter.16.cloned.1.call-update) | async-done | bytes 786448 | tf_op jit(solution)/shard_map/reduce_scatter | solution.py:251
  766.8 8.1 convolution_convert_fusion.5
  775.0 8.3 convolution_convert_fusion.6
  783.4 8.3 convolution_convert_fusion.7
  791.8 73.2 %all-gather.19.cloned.1.call-done = bf16[3072,1024]{1,0:T(8,128)(2,1)} async-done(((bf16[384,1024]{1,0:T(8,128)(2,1)}), bf16[3072,1024]{1,0:T(8,128)(2,1)}) %all-gather.19.cloned.1.call-update) | async-done | bytes 6291472 | tf_op jit(solution)/shard_map/all_gather | solution.py:264
  869.7 6.1 convolution_convert_fusion.1
  876.7 201.5 %while.28 = (s32[]{:T(128)}, f32[3072,2,64]{0,2,1:T(8,128)S(1)}, f32[3072,2,64]{0,2,1:T(8,128)}, bf16[6,512,2,64]{1,3,2,0:T(8,128)(2,1)}, s32[6]{0:T(128)S(1)}, ...) while((s32[]{:T(128)}, f32[3072,2,64]{0,2,1:T(8,128)S(1)}, ...), condition=%wide.region_12.13_spmd.clone, body=%wide.region_10.12_spmd.clone.sunk | while | flops 2067266560 | bytes 122618160 | solution.py:96
  889.1 8.9 multiply_reduce_fusion.3
  898.1 7.6 multiply_convert_fusion.7
  922.7 8.9 multiply_reduce_fusion.3
  931.6 7.6 multiply_convert_fusion.7
  956.3 8.9 multiply_reduce_fusion.3
  965.3 7.5 multiply_convert_fusion.7
  989.8 8.9 multiply_reduce_fusion.3
  998.7 7.5 multiply_convert_fusion.7
  1023.3 8.9 multiply_reduce_fusion.3
  1032.2 7.5 multiply_convert_fusion.7
  1056.7 8.8 multiply_reduce_fusion.3
  1065.6 7.5 multiply_convert_fusion.7
  1081.2 5.5 convolution_convert_fusion.11
  1086.8 7.7 fusion.63
  1097.1 6.4 fusion.62
  1103.6 5.3 convolution_convert_fusion.9
  1109.0 12.2 add_convert_fusion
  1122.5 7.5 convolution_convert_fusion
  1140.2 10.2 reduce-scatter.24.cloned.1.call-done
  1151.9 120.2 %reduce-scatter.18.cloned.1.call-done = bf16[384,1024]{1,0:T(8,128)(2,1)} async-done(((bf16[3072,1024]{1,0:T(8,128)(2,1)}), bf16[384,1024]{1,0:T(8,128)(2,1)}) %reduce-scatter.18.cloned.1.call-update) | async-done | bytes 786448 | tf_op jit(solution)/shard_map/reduce_scatter | solution.py:307
  1273.7 42.1 %all-reduce.2 = (f32[1024]{0:T(1024)S(1)}, f32[1024]{0:T(1024)S(1)}) all-reduce(f32[1024]{0:T(1024)S(1)} %get-tuple-element.169, f32[1024]{0:T(1024)S(1)} %copy-done.31), channel_id=13, replica_groups=mesh['dp'=4,'tensor'=8] {'dp','tensor'}, use_global_device_ids=true, to_apply=%region_23.24.clone | all-reduce | flops 2048 | bytes 16384
  1317.0 77.0 %reduce-scatter.14.cloned.1.call-done = bf16[384,1024]{1,0:T(8,128)(2,1)} async-done(((bf16[3072,1024]{1,0:T(8,128)(2,1)}), bf16[384,1024]{1,0:T(8,128)(2,1)}) %reduce-scatter.14.cloned.1.call-update) | async-done | bytes 786448 | tf_op jit(solution)/shard_map/reduce_scatter | solution.py:207
  (307 shorter events, 255.7 us)
Async XLA Ops:
  8.0 111.9 %all-gather.9.cloned.1.call-start = ((), (), s32[]{:S(2)}) async-start(), calls=%async_computation.11 | async-start | bytes 7077888 | tf_op jit(solution)/shard_map/all_gather | solution.py:146
  10.7 14.8 %copy-start.25 = (f32[384]{0:T(512)}, f32[384]{0:T(512)S(1)}, u32[]{:S(2)}) copy-start(f32[384]{0:T(512)S(1)} %get-tuple-element.229) | copy-start | bytes 4612
  18.9 457.7 %reduce-scatter.12.cloned.1.call-start = ((), (), s32[]{:S(2)}) async-start(), calls=%async_computation.12 | async-start | bytes 14155776 | tf_op jit(solution)/shard_map/reduce_scatter | solution.py:166
  25.5 101.8 %copy-start.10 = (bf16[1024,128]{1,0:T(8,128)(2,1)}, bf16[1024,128]{1,0:T(8,128)(2,1)S(1)}, u32[]{:S(2)}) copy-start(bf16[1024,128]{1,0:T(8,128)(2,1)S(1)} %all_gather.47) | copy-start | bytes 786436
  31.6 93.5 %copy-start.12 = (bf16[1024,128]{1,0:T(8,128)(2,1)}, bf16[1024,128]{1,0:T(8,128)(2,1)S(1)}, u32[]{:S(2)}) copy-start(bf16[1024,128]{1,0:T(8,128)(2,1)S(1)} %all_gather.48) | copy-start | bytes 786436
  37.7 82.3 %copy-start.8 = (bf16[1024,128]{1,0:T(8,128)(2,1)}, bf16[1024,128]{1,0:T(8,128)(2,1)S(1)}, u32[]{:S(2)}) copy-start(bf16[1024,128]{1,0:T(8,128)(2,1)S(1)} %all_gather.49) | copy-start | bytes 786436
  225.7 333.2 %all-gather.15.cloned.1.call-start = ((), (), s32[]{:S(2)}) async-start(), calls=%async_computation.15 | async-start | bytes 1310720 | tf_op jit(solution)/shard_map/all_gather | solution.py:129
  226.3 332.7 %all-gather.17.cloned.1.call-start = ((), (), s32[]{:S(2)}) async-start(), calls=%async_computation.17 | async-start | bytes 7077888 | tf_op jit(solution)/shard_map/all_gather | solution.py:238
  226.9 385.5 %all-gather.13.cloned.1.call-start = ((), (), s32[]{:S(2)}) async-start(), calls=%async_computation.14 | async-start | bytes 1310720 | tf_op jit(solution)/shard_map/all_gather | solution.py:128
  227.5 394.1 %all-gather.11.cloned.1.call-start = ((), (), s32[]{:S(2)}) async-start(), calls=%async_computation.13 | async-start | bytes 1310720 | tf_op jit(solution)/shard_map/all_gather | solution.py:127
  232.6 530.8 %copy-start.19 = (f32[4,1,256]{2,1,0:T(1,128)}, f32[4,1,256]{2,1,0:T(1,128)S(1)}, u32[]{:S(2)}) copy-start(f32[4,1,256]{2,1,0:T(1,128)S(1)} %convert_element_type.176) | copy-start | bytes 12292
  478.5 284.9 %copy-start.1 = (f32[384,1024]{1,0:T(8,128)}, f32[384,1024]{1,0:T(8,128)S(1)}, u32[]{:S(2)}) copy-start(f32[384,1024]{1,0:T(8,128)S(1)} %get-tuple-element.218) | copy-start | bytes 4718596
  478.5 284.9 %copy-start.23 = (f32[384]{0:T(512)}, f32[384]{0:T(512)S(1)}, u32[]{:S(2)}) copy-start(f32[384]{0:T(512)S(1)} %get-tuple-element.231) | copy-start | bytes 4612
  478.6 284.9 %copy-start.27 = (f32[384]{0:T(512)}, f32[384]{0:T(512)S(1)}, u32[]{:S(2)}) copy-start(f32[384]{0:T(512)S(1)} %get-tuple-element.230) | copy-start | bytes 4612
  483.2 35.3 %collective-permute-start = (bf16[384,1024]{1,0:T(8,128)(2,1)S(1)}, bf16[384,1024]{1,0:T(8,128)(2,1)}, u32[]{:S(2)}, u32[]{:S(2)}) collective-permute-start(bf16[384,1024]{1,0:T(8,128)(2,1)S(1)} %get-tuple-element.216), channel_id=1, source_target_pairs={{0,1},{1,2},{2,3},{3,4},{4,5},{5,6},{6,7},{7,0},{8,9},{9,10},{10,1... | collective-permute-start | bytes 2359304 | tf_op jit(solution)/shard_map/ppermute | solution.py:191
  484.7 36.3 %collective-permute-start.1 = (bf16[384,1024]{1,0:T(8,128)(2,1)S(1)}, bf16[384,1024]{1,0:T(8,128)(2,1)}, u32[]{:S(2)}, u32[]{:S(2)}) collective-permute-start(bf16[384,1024]{1,0:T(8,128)(2,1)S(1)} %get-tuple-element.216), channel_id=1, source_target_pairs={{0,7},{1,0},{2,1},{3,2},{4,3},{5,4},{6,5},{7,6},{8,15},{9,8},{10,9... | collective-permute-start | bytes 2359304 | tf_op jit(solution)/shard_map/ppermute | solution.py:196
  518.4 35.8 %collective-permute-start.2 = (bf16[384,1024]{1,0:T(8,128)(2,1)}, bf16[384,1024]{1,0:T(8,128)(2,1)}, u32[]{:S(2)}, u32[]{:S(2)}) collective-permute-start(bf16[384,1024]{1,0:T(8,128)(2,1)} %collective-permute-done), channel_id=1, source_target_pairs={{0,1},{1,2},{2,3},{3,4},{4,5},{5,6},{6,7},{7,0},{8,9},{9,10},{10,1... | collective-permute-start | bytes 2359304 | tf_op jit(solution)/shard_map/ppermute | solution.py:191
  521.0 35.7 %collective-permute-start.3 = (bf16[384,1024]{1,0:T(8,128)(2,1)}, bf16[384,1024]{1,0:T(8,128)(2,1)}, u32[]{:S(2)}, u32[]{:S(2)}) collective-permute-start(bf16[384,1024]{1,0:T(8,128)(2,1)} %collective-permute-done.1), channel_id=1, source_target_pairs={{0,7},{1,0},{2,1},{3,2},{4,3},{5,4},{6,5},{7,6},{8,15},{9,8},{10,9... | collective-permute-start | bytes 2359304 | tf_op jit(solution)/shard_map/ppermute | solution.py:196
  523.2 238.1 %reduce-scatter.16.cloned.1.call-start = ((), (), s32[]{:S(2)}) async-start(), calls=%async_computation.18 | async-start | bytes 7077888 | tf_op jit(solution)/shard_map/reduce_scatter | solution.py:251
  554.3 35.7 %collective-permute-start.4 = (bf16[384,1024]{1,0:T(8,128)(2,1)}, bf16[384,1024]{1,0:T(8,128)(2,1)}, u32[]{:S(2)}, u32[]{:S(2)}) collective-permute-start(bf16[384,1024]{1,0:T(8,128)(2,1)} %collective-permute-done.2), channel_id=1, source_target_pairs={{0,1},{1,2},{2,3},{3,4},{4,5},{5,6},{6,7},{7,0},{8,9},{9,10},{10,1... | collective-permute-start | bytes 2359304 | tf_op jit(solution)/shard_map/ppermute | solution.py:191
  556.7 46.4 %collective-permute-start.5 = (bf16[384,1024]{1,0:T(8,128)(2,1)}, bf16[384,1024]{1,0:T(8,128)(2,1)}, u32[]{:S(2)}, u32[]{:S(2)}) collective-permute-start(bf16[384,1024]{1,0:T(8,128)(2,1)} %collective-permute-done.3), channel_id=1, source_target_pairs={{0,7},{1,0},{2,1},{3,2},{4,3},{5,4},{6,5},{7,6},{8,15},{9,8},{10,9... | collective-permute-start | bytes 2359304 | tf_op jit(solution)/shard_map/ppermute | solution.py:196
  589.9 21.5 %collective-permute-start.6 = (bf16[384,1024]{1,0:T(8,128)(2,1)}, bf16[384,1024]{1,0:T(8,128)(2,1)S(1)}, u32[]{:S(2)}, u32[]{:S(2)}) collective-permute-start(bf16[384,1024]{1,0:T(8,128)(2,1)} %collective-permute-done.4), channel_id=1, source_target_pairs={{0,1},{1,2},{2,3},{3,4},{4,5},{5,6},{6,7},{7,0},{8,9},{9,10},{10,1... | collective-permute-start | bytes 2359304 | tf_op jit(solution)/shard_map/ppermute | solution.py:191
  621.6 13.5 copy-start.35
  646.3 218.6 %all-gather.19.cloned.1.call-start = ((), (), s32[]{:S(2)}) async-start(), calls=%async_computation.19 | async-start | bytes 7077888 | tf_op jit(solution)/shard_map/all_gather | solution.py:264
  766.8 363.3 %reduce-scatter.32.cloned.1.call-start = ((), (), s32[]{:S(2)}) async-start(), calls=%async_computation.27 | async-start | bytes 1310720 | tf_op jit(solution)/shard_map/reduce_scatter | solution.py:300
  775.0 357.1 %reduce-scatter.30.cloned.1.call-start = ((), (), s32[]{:S(2)}) async-start(), calls=%async_computation.26 | async-start | bytes 1310720 | tf_op jit(solution)/shard_map/reduce_scatter | solution.py:297
  783.3 350.5 %reduce-scatter.28.cloned.1.call-start = ((), (), s32[]{:S(2)}) async-start(), calls=%async_computation.25 | async-start | bytes 1310720 | tf_op jit(solution)/shard_map/reduce_scatter | solution.py:294
  791.7 344.0 %reduce-scatter.26.cloned.1.call-start = ((), (), s32[]{:S(2)}) async-start(), calls=%async_computation.24 | async-start | bytes 327680 | tf_op jit(solution)/shard_map/reduce_scatter | solution.py:291
  869.7 267.5 %reduce-scatter.20.cloned.1.call-start = ((), (), s32[]{:S(2)}) async-start(), calls=%async_computation.21 | async-start | bytes 327680 | tf_op jit(solution)/shard_map/reduce_scatter | solution.py:282
  956.3 8.9 copy-start.17
  989.8 8.9 copy-start.17
  1023.3 8.9 copy-start.17
  1081.2 13.3 slice-start
  1086.7 52.0 %reduce-scatter.22.cloned.1.call-start = ((), (), s32[]{:S(2)}) async-start(), calls=%async_computation.22 | async-start | bytes 327680 | tf_op jit(solution)/shard_map/reduce_scatter | solution.py:285
  1097.1 53.3 %reduce-scatter.24.cloned.1.call-start = ((), (), s32[]{:S(2)}) async-start(), calls=%async_computation.23 | async-start | bytes 327680 | tf_op jit(solution)/shard_map/reduce_scatter | solution.py:288
  1109.0 163.1 %reduce-scatter.18.cloned.1.call-start = ((), (), s32[]{:S(2)}) async-start(), calls=%async_computation.20 | async-start | bytes 7077888 | tf_op jit(solution)/shard_map/reduce_scatter | solution.py:307
  1121.3 272.7 %reduce-scatter.14.cloned.1.call-start = ((), (), s32[]{:S(2)}) async-start(), calls=%async_computation.16 | async-start | bytes 7077888 | tf_op jit(solution)/shard_map/reduce_scatter | solution.py:207
  1130.0 142.1 %copy-start.3 = (bf16[384,1024]{1,0:T(8,128)(2,1)S(1)}, bf16[384,1024]{1,0:T(8,128)(2,1)}, u32[]{:S(2)}) copy-start(bf16[384,1024]{1,0:T(8,128)(2,1)} %param.17) | copy-start | bytes 2359300
  1130.0 142.1 %copy-start.22 = (f32[4,1,256]{2,1,0:T(1,128)S(1)}, f32[4,1,256]{2,1,0:T(1,128)}, u32[]{:S(2)}) copy-start(f32[4,1,256]{2,1,0:T(1,128)} %copy-done.21) | copy-start | bytes 12292
  1130.0 142.1 %copy-start.26 = (f32[384]{0:T(512)S(1)}, f32[384]{0:T(512)}, u32[]{:S(2)}) copy-start(f32[384]{0:T(512)} %copy-done.25) | copy-start | bytes 4612
  1130.0 143.7 %copy-start.31 = (f32[1024]{0:T(1024)S(1)}, f32[1024]{0:T(1024)}, u32[]{:S(2)}) copy-start(f32[1024]{0:T(1024)} %get-tuple-element.167) | copy-start | bytes 12292
  1130.0 264.0 %copy-start.2 = (f32[384,1024]{1,0:T(8,128)S(1)}, f32[384,1024]{1,0:T(8,128)}, u32[]{:S(2)}) copy-start(f32[384,1024]{1,0:T(8,128)} %copy-done.1) | copy-start | bytes 4718596
  1130.0 264.0 %copy-start.6 = (bf16[384,1024]{1,0:T(8,128)(2,1)S(1)}, bf16[384,1024]{1,0:T(8,128)(2,1)}, u32[]{:S(2)}) copy-start(bf16[384,1024]{1,0:T(8,128)(2,1)} %param.29) | copy-start | bytes 2359300
  1130.0 263.9 %copy-start.20 = (f32[4,1,256]{2,1,0:T(1,128)S(1)}, f32[4,1,256]{2,1,0:T(1,128)}, u32[]{:S(2)}) copy-start(f32[4,1,256]{2,1,0:T(1,128)} %copy-done.19) | copy-start | bytes 12292
  1130.0 263.9 %copy-start.24 = (f32[384]{0:T(512)S(1)}, f32[384]{0:T(512)}, u32[]{:S(2)}) copy-start(f32[384]{0:T(512)} %copy-done.23) | copy-start | bytes 4612
  1130.0 263.9 %copy-start.28 = (f32[384]{0:T(512)S(1)}, f32[384]{0:T(512)}, u32[]{:S(2)}) copy-start(f32[384]{0:T(512)} %copy-done.27) | copy-start | bytes 4612
  1130.1 263.9 %copy-start.30 = (f32[384]{0:T(512)S(1)}, f32[384]{0:T(512)}, u32[]{:S(2)}) copy-start(f32[384]{0:T(512)} %copy-done.29) | copy-start | bytes 4612
  1130.1 263.9 %copy-start.32 = (f32[384]{0:T(512)S(1)}, f32[384]{0:T(512)}, u32[]{:S(2)}) copy-start(f32[384]{0:T(512)} %get-tuple-element.228) | copy-start | bytes 4612
  (26 other events, 124.4 us)
Sparse Core Ops, SparseCore 0:
  19.1 100.8 all-gather.8
  225.9 250.7 reduce-scatter.11
Sparse Core Ops, SparseCore 1:
  227.8 14.9 all-gather.14
  244.8 168.4 all-gather.16
  414.6 15.6 all-gather.12
  523.3 14.1 all-gather.10
  646.4 114.8 reduce-scatter.15
  766.9 98.0 all-gather.18
  867.3 22.9 reduce-scatter.31
  892.9 24.8 reduce-scatter.29
  920.1 24.8 reduce-scatter.27
  947.6 19.9 reduce-scatter.25
  1086.7 18.0 reduce-scatter.19
  1108.0 19.9 reduce-scatter.21
  1130.3 20.0 reduce-scatter.23
  1154.4 117.6 reduce-scatter.17
  1276.1 117.8 reduce-scatter.13
